TPU v7x, 32 devices: a whole 2x2x4 slice. The times are simulated.
32 devices in a mesh: seq: 4 (over x, core), clip: 8 (over z, y).
Axes of the slice: x: 2, y: 2, z: 4, core: 2. Of those that a mesh axis runs over, the one named last changes fastest.
Arguments:
- patches: bfloat16 [64, 8, 64, 768], P('clip', None, 'seq'), may hold values from -6 to 6
- mask_index: int32 [64, 450], P('clip'), may hold values from 0 to 511, as said below
- mask_count: int32 [64], P('clip'), may hold values from 100 to 450, as said below
- cotangent: bfloat16 [64, 8, 64, 768], P('clip', None, 'seq'), may hold values from -6 to 6
- w_qkv: bfloat16 [768, 2304], P(('seq', 'clip')), may hold values from -0.3125 to 0.3125
- w_out: bfloat16 [768, 768], P(('seq', 'clip')), may hold values from -0.4375 to 0.4375
- mask_embed: bfloat16 [768], P(('seq', 'clip')), may hold values from -5 to 5
- gains: bfloat16 [2, 768], P(None, ('seq', 'clip')), may hold values from 0.5 to 1.5
- biases: bfloat16 [6, 768], P(None, ('seq', 'clip')), may hold values from -0.5 to 0.5
- w_up: bfloat16 [768, 3072], P(('seq', 'clip')), may hold values from -0.21875 to 0.21875
- w_down: bfloat16 [3072, 768], P(('seq', 'clip')), may hold values from -0.109375 to 0.109375
- up_bias: bfloat16 [3072], P(('seq', 'clip')), may hold values from -2.5 to 2.5
- avg_qkv: float32 [768, 2304], P(('seq', 'clip')), may hold values from -0.3125 to 0.3125
- avg_out: float32 [768, 768], P(('seq', 'clip')), may hold values from -0.4375 to 0.4375
- avg_mask: float32 [768], P(('seq', 'clip')), may hold values from -5 to 5
- avg_gains: float32 [2, 768], P(None, ('seq', 'clip')), may hold values from -1 to 1
- avg_biases: float32 [6, 768], P(None, ('seq', 'clip')), may hold values from -0.5 to 0.5
- avg_up: float32 [768, 3072], P(('seq', 'clip')), may hold values from -0.21875 to 0.21875
- avg_down: float32 [3072, 768], P(('seq', 'clip')), may hold values from -0.109375 to 0.109375
- avg_up_bias: float32 [3072], P(('seq', 'clip')), may hold values from -2.5 to 2.5
Outputs:
- activations: bfloat16 [64, 8, 64, 768], P('clip', None, 'seq')
- input_grad: bfloat16 [64, 8, 64, 768], P('clip', None, 'seq')
- grad_qkv: float32 [768, 2304], P(('seq', 'clip'))
- grad_out: float32 [768, 768], P(('seq', 'clip'))
- grad_mask: float32 [768], P(('seq', 'clip'))
- grad_gains: float32 [2, 768], P(None, ('seq', 'clip'))
- grad_biases: float32 [6, 768], P(None, ('seq', 'clip'))
- grad_up: float32 [768, 3072], P(('seq', 'clip'))
- grad_down: float32 [3072, 768], P(('seq', 'clip'))
- grad_up_bias: float32 [3072], P(('seq', 'clip'))
- new_qkv: float32 [768, 2304], P(('seq', 'clip'))
- new_out: float32 [768, 768], P(('seq', 'clip'))
- new_mask: float32 [768], P(('seq', 'clip'))
- new_gains: float32 [2, 768], P(None, ('seq', 'clip'))
- new_biases: float32 [6, 768], P(None, ('seq', 'clip'))
- new_up: float32 [768, 3072], P(('seq', 'clip'))
- new_down: float32 [3072, 768], P(('seq', 'clip'))
- new_up_bias: float32 [3072], P(('seq', 'clip'))
Inputs may be any that keep to these rules, and one draw needn't show every extreme that they name: `mask_index`: each row holds 450 different patch numbers of its clip; only its first mask_count entries are masked, the others are to be ignored. `mask_count`: some clip has exactly 450 masked patches in every draw.
All inputs are finite; a program needn't handle non-finite values.
Results may differ from a plain program's by a relative error of at most 0.015.
Values may be sent and summed in bfloat16 or wider, within the bound.
No kernel may reach another device: no remote copies, remote signals or barrier semaphores. Data moves between devices by JAX's collectives and lax.ppermute only.
A program may use at most 192 MiB of HBM per device.

v0:
```python
from functools import partial
import math
import jax
import jax.numpy as jnp
from jax import lax
from jax.sharding import PartitionSpec as P

H = 12
norm_eps = 1e-06


def layer_norm(hidden, gain_row, shift_row):
    center = hidden - jnp.mean(hidden, axis=-1, keepdims=True)
    spread = jnp.mean(center * center, axis=-1, keepdims=True)
    return center * lax.rsqrt(spread + norm_eps) * gain_row + shift_row


def exact_gelu(upper_rows):
    return jax.nn.gelu(upper_rows, approximate=False)


def row_product(left_side, right_side):
    return lax.dot_general(
        left_side, right_side, (((0,), (0,)), ((), ())), preferred_element_type=jnp.float32
    )


def back_product(left_side, right_side):
    return lax.dot_general(
        left_side, right_side, (((1,), (1,)), ((), ())), preferred_element_type=jnp.float32
    )


def split_heads(array_rows, head_count):
    clip_count, row_count, model_width = array_rows.shape
    return array_rows.reshape(clip_count, row_count, head_count, model_width // head_count)


def make_groups(array_rows, group_size):
    return array_rows.reshape(
        (array_rows.shape[0] // group_size, group_size) + array_rows.shape[1:]
    )


def attend_forward(operands, head_count, score_scale):
    queries, keys_all, values_all = operands
    clip_count, query_rows, model_width = queries.shape
    query_h = split_heads(queries, head_count)
    key_h = split_heads(keys_all, head_count)
    value_h = split_heads(values_all, head_count)
    scores = (
        jnp.einsum("cqhd,ckhd->chqk", query_h, key_h, preferred_element_type=jnp.float32)
        * score_scale
    )
    row_max = jnp.max(scores, axis=-1, keepdims=True)
    shifted = jnp.exp(scores - row_max)
    row_sum = jnp.sum(shifted, axis=-1, keepdims=True)
    attn_prob = shifted / row_sum
    mixed_rows = jnp.einsum(
        "chqk,ckhd->cqhd",
        attn_prob.astype(jnp.bfloat16),
        value_h,
        preferred_element_type=jnp.float32,
    )
    log_total = (row_max + jnp.log(row_sum))[..., 0]
    return (mixed_rows.reshape(clip_count, query_rows, model_width).astype(jnp.bfloat16), log_total)


def attend_backward(operands, head_count, score_scale):
    queries, keys_all, values_all, grad_mixed, log_total = operands
    clip_count, query_rows, model_width = queries.shape
    key_rows = keys_all.shape[1]
    query_h = split_heads(queries, head_count)
    key_h = split_heads(keys_all, head_count)
    value_h = split_heads(values_all, head_count)
    grad_heads = split_heads(grad_mixed, head_count)
    scores = (
        jnp.einsum("cqhd,ckhd->chqk", query_h, key_h, preferred_element_type=jnp.float32)
        * score_scale
    )
    attn_prob = jnp.exp(scores - log_total[..., None])
    grad_prob = jnp.einsum(
        "cqhd,ckhd->chqk", grad_heads, value_h, preferred_element_type=jnp.float32
    )
    inner_sum = jnp.sum(grad_prob * attn_prob, axis=-1, keepdims=True)
    grad_scores = (attn_prob * (grad_prob - inner_sum)).astype(jnp.bfloat16)
    grad_query = (
        jnp.einsum("chqk,ckhd->cqhd", grad_scores, key_h, preferred_element_type=jnp.float32)
        * score_scale
    )
    grad_key = (
        jnp.einsum("chqk,cqhd->ckhd", grad_scores, query_h, preferred_element_type=jnp.float32)
        * score_scale
    )
    grad_value = jnp.einsum(
        "chqk,cqhd->ckhd",
        attn_prob.astype(jnp.bfloat16),
        grad_heads,
        preferred_element_type=jnp.float32,
    )
    grad_query = grad_query.reshape(clip_count, query_rows, model_width).astype(jnp.bfloat16)
    grad_key = grad_key.reshape(clip_count, key_rows, model_width)
    grad_value = grad_value.reshape(clip_count, key_rows, model_width)
    return (grad_query, grad_key, grad_value)


def body(
    patches,
    mask_index,
    mask_count,
    cotangent,
    w_qkv,
    w_out,
    mask_embed,
    gains,
    biases,
    w_up,
    w_down,
    up_bias,
    avg_qkv,
    avg_out,
    avg_mask,
    avg_gains,
    avg_biases,
    avg_up,
    avg_down,
    avg_up_bias,
):
    clip_count, freq_rows, time_local, model_width = patches.shape
    seq_size = lax.axis_size("seq")
    time_total = time_local * seq_size
    length = freq_rows * time_total
    local_len = freq_rows * time_local
    row_total = clip_count * local_len
    head_count = H
    score_scale = 1.0 / math.sqrt(model_width // head_count)
    forward_fn = partial(attend_forward, head_count=head_count, score_scale=score_scale)
    backward_fn = partial(attend_backward, head_count=head_count, score_scale=score_scale)
    gathered = (
        lax.all_gather(w_qkv, ("seq", "clip"), axis=0, tiled=True),
        lax.all_gather(w_out, ("seq", "clip"), axis=0, tiled=True),
        lax.all_gather(mask_embed, ("seq", "clip"), axis=0, tiled=True),
        lax.all_gather(gains, ("seq", "clip"), axis=1, tiled=True),
        lax.all_gather(biases, ("seq", "clip"), axis=1, tiled=True),
        lax.all_gather(w_up, ("seq", "clip"), axis=0, tiled=True),
        lax.all_gather(w_down, ("seq", "clip"), axis=0, tiled=True),
        lax.all_gather(up_bias, ("seq", "clip"), axis=0, tiled=True),
    )
    full_qkv, full_out, full_mask, full_gains, full_biases, full_up, full_down, full_up_bias = (
        gathered
    )
    gain_rows = full_gains.astype(jnp.float32)
    bias_rows = full_biases.astype(jnp.float32)
    mask_vector = full_mask.astype(jnp.float32)
    up_shift = full_up_bias.astype(jnp.float32)
    freq_ids = lax.broadcasted_iota(jnp.int32, (freq_rows, time_local), 0)
    time_ids = (
        lax.broadcasted_iota(jnp.int32, (freq_rows, time_local), 1)
        + lax.axis_index("seq") * time_local
    )
    positions = (freq_ids * time_total + time_ids).reshape(local_len)
    slot_ids = lax.broadcasted_iota(jnp.int32, mask_index.shape, 1)
    slot_live = slot_ids < mask_count[:, None]
    slot_hits = (mask_index[:, :, None] == positions[None, None, :]) & slot_live[:, :, None]
    masked = jnp.any(slot_hits, axis=1).reshape(row_total, 1)
    fresh_rows = patches.reshape(row_total, model_width).astype(jnp.float32)
    start_rows = jnp.where(masked, mask_vector, fresh_rows)
    normed_one, norm_pull_one = jax.vjp(layer_norm, start_rows, gain_rows[0], bias_rows[0])
    normed_low = normed_one.astype(jnp.bfloat16)
    joined = jnp.dot(normed_low, full_qkv, preferred_element_type=jnp.float32)
    queries = (joined[:, :model_width] + bias_rows[1]).astype(jnp.bfloat16)
    keys_loc = joined[:, model_width : 2 * model_width].astype(jnp.bfloat16)
    values_loc = (joined[:, 2 * model_width :] + bias_rows[2]).astype(jnp.bfloat16)
    grid_shape = (clip_count, freq_rows, time_local, model_width)
    key_grid = keys_loc.reshape(grid_shape)
    value_grid = values_loc.reshape(grid_shape)
    key_all, value_all = (
        lax.all_gather(key_grid, "seq", axis=2, tiled=True),
        lax.all_gather(value_grid, "seq", axis=2, tiled=True),
    )
    group_size = math.gcd(clip_count, max(1, 512 // local_len))
    query_groups = make_groups(queries.reshape(clip_count, local_len, model_width), group_size)
    key_groups = make_groups(key_all.reshape(clip_count, length, model_width), group_size)
    value_groups = make_groups(value_all.reshape(clip_count, length, model_width), group_size)
    mixed_groups, log_groups = lax.map(forward_fn, (query_groups, key_groups, value_groups))
    mixed_flat = mixed_groups.reshape(row_total, model_width)
    middle = start_rows + (
        jnp.dot(mixed_flat, full_out, preferred_element_type=jnp.float32) + bias_rows[3]
    )
    normed_two, norm_pull_two = jax.vjp(layer_norm, middle, gain_rows[1], bias_rows[4])
    second_low = normed_two.astype(jnp.bfloat16)
    upper_rows = jnp.dot(second_low, full_up, preferred_element_type=jnp.float32) + up_shift
    active, gelu_pull = jax.vjp(exact_gelu, upper_rows)
    active_low = active.astype(jnp.bfloat16)
    final_rows = middle + (
        jnp.dot(active_low, full_down, preferred_element_type=jnp.float32) + bias_rows[5]
    )
    activations = final_rows.astype(jnp.bfloat16).reshape(patches.shape)
    grad_final = cotangent.reshape(row_total, model_width)
    grad_down_part = row_product(active_low, grad_final)
    grad_down_bias = jnp.sum(grad_final.astype(jnp.float32), axis=0)
    grad_active = back_product(grad_final, full_down)
    (grad_upper,) = gelu_pull(grad_active)
    grad_upper_low = grad_upper.astype(jnp.bfloat16)
    grad_up_part = row_product(second_low, grad_upper_low)
    grad_up_shift = jnp.sum(grad_upper_low.astype(jnp.float32), axis=0)
    grad_second = back_product(grad_upper_low, full_up)
    grad_mid_norm, grad_gain_two, grad_bias_two = norm_pull_two(grad_second)
    grad_middle = grad_final.astype(jnp.float32) + grad_mid_norm
    grad_branch = grad_middle.astype(jnp.bfloat16)
    grad_out_part = row_product(mixed_flat, grad_branch)
    grad_out_bias = jnp.sum(grad_branch.astype(jnp.float32), axis=0)
    grad_mixed = back_product(grad_branch, full_out).astype(jnp.bfloat16)
    grad_mixed_groups = make_groups(
        grad_mixed.reshape(clip_count, local_len, model_width), group_size
    )
    grad_query_groups, grad_key_groups, grad_value_groups = lax.map(
        backward_fn, (query_groups, key_groups, value_groups, grad_mixed_groups, log_groups)
    )
    grad_key_own, grad_value_own = (
        lax.psum_scatter(
            grad_key_groups.reshape(clip_count, freq_rows, time_total, model_width).astype(
                jnp.bfloat16
            ),
            "seq",
            scatter_dimension=2,
            tiled=True,
        ).astype(jnp.float32),
        lax.psum_scatter(
            grad_value_groups.reshape(clip_count, freq_rows, time_total, model_width).astype(
                jnp.bfloat16
            ),
            "seq",
            scatter_dimension=2,
            tiled=True,
        ).astype(jnp.float32),
    )
    grad_query_loc = grad_query_groups.reshape(row_total, model_width)
    grad_key_loc = grad_key_own.reshape(row_total, model_width).astype(jnp.bfloat16)
    grad_value_loc = grad_value_own.reshape(row_total, model_width).astype(jnp.bfloat16)
    grad_joined = jnp.concatenate([grad_query_loc, grad_key_loc, grad_value_loc], axis=1)
    grad_qkv_part = row_product(normed_low, grad_joined)
    grad_query_bias = jnp.sum(grad_query_loc.astype(jnp.float32), axis=0)
    grad_value_bias = jnp.sum(grad_value_loc.astype(jnp.float32), axis=0)
    grad_first = back_product(grad_joined, full_qkv)
    grad_start_norm, grad_gain_one, grad_bias_one = norm_pull_one(grad_first)
    grad_start = grad_middle + grad_start_norm
    input_grad = jnp.where(masked, 0.0, grad_start).astype(jnp.bfloat16).reshape(patches.shape)
    grad_mask_part = jnp.sum(jnp.where(masked, grad_start, 0.0), axis=0)
    grad_gain_part = jnp.stack([grad_gain_one, grad_gain_two])
    grad_bias_part = jnp.stack(
        [
            grad_bias_one,
            grad_query_bias,
            grad_value_bias,
            grad_out_bias,
            grad_bias_two,
            grad_down_bias,
        ]
    )
    summed = (
        lax.psum_scatter(grad_qkv_part, ("seq", "clip"), scatter_dimension=0, tiled=True),
        lax.psum_scatter(grad_out_part, ("seq", "clip"), scatter_dimension=0, tiled=True),
        lax.psum_scatter(grad_mask_part, ("seq", "clip"), scatter_dimension=0, tiled=True),
        lax.psum_scatter(grad_gain_part, ("seq", "clip"), scatter_dimension=1, tiled=True),
        lax.psum_scatter(grad_bias_part, ("seq", "clip"), scatter_dimension=1, tiled=True),
        lax.psum_scatter(grad_up_part, ("seq", "clip"), scatter_dimension=0, tiled=True),
        lax.psum_scatter(grad_down_part, ("seq", "clip"), scatter_dimension=0, tiled=True),
        lax.psum_scatter(grad_up_shift, ("seq", "clip"), scatter_dimension=0, tiled=True),
    )
    new_qkv = 0.9 * avg_qkv + 0.1 * w_qkv.astype(jnp.float32)
    new_out = 0.9 * avg_out + 0.1 * w_out.astype(jnp.float32)
    new_mask = 0.9 * avg_mask + 0.1 * mask_embed.astype(jnp.float32)
    new_gains = 0.9 * avg_gains + 0.1 * gains.astype(jnp.float32)
    new_biases = 0.9 * avg_biases + 0.1 * biases.astype(jnp.float32)
    new_up = 0.9 * avg_up + 0.1 * w_up.astype(jnp.float32)
    new_down = 0.9 * avg_down + 0.1 * w_down.astype(jnp.float32)
    new_up_bias = 0.9 * avg_up_bias + 0.1 * up_bias.astype(jnp.float32)
    return (
        activations,
        input_grad,
        summed[0],
        summed[1],
        summed[2],
        summed[3],
        summed[4],
        summed[5],
        summed[6],
        summed[7],
        new_qkv,
        new_out,
        new_mask,
        new_gains,
        new_biases,
        new_up,
        new_down,
        new_up_bias,
    )


def solution(mesh):
    placed = (
        P("clip", None, "seq", None),
        P("clip", None),
        P("clip"),
        P("clip", None, "seq", None),
        P(("seq", "clip"), None),
        P(("seq", "clip"), None),
        P(("seq", "clip")),
        P(None, ("seq", "clip")),
        P(None, ("seq", "clip")),
        P(("seq", "clip"), None),
        P(("seq", "clip"), None),
        P(("seq", "clip")),
        P(("seq", "clip"), None),
        P(("seq", "clip"), None),
        P(("seq", "clip")),
        P(None, ("seq", "clip")),
        P(None, ("seq", "clip")),
        P(("seq", "clip"), None),
        P(("seq", "clip"), None),
        P(("seq", "clip")),
    )
    return jax.shard_map(
        body,
        mesh=mesh,
        in_specs=placed,
        out_specs=(
            P("clip", None, "seq", None),
            P("clip", None, "seq", None),
            P(("seq", "clip"), None),
            P(("seq", "clip"), None),
            P(("seq", "clip")),
            P(None, ("seq", "clip")),
            P(None, ("seq", "clip")),
            P(("seq", "clip"), None),
            P(("seq", "clip"), None),
            P(("seq", "clip")),
            P(("seq", "clip"), None),
            P(("seq", "clip"), None),
            P(("seq", "clip")),
            P(None, ("seq", "clip")),
            P(None, ("seq", "clip")),
            P(("seq", "clip"), None),
            P(("seq", "clip"), None),
            P(("seq", "clip")),
        ),
        check_vma=False,
    )
```

profile of v0, /device:TPU:0, one launch (start us, length us, event | category | flops | bytes accessed | tf_op | source)
XLA Modules:
  0.0 1272.0 jit_solution(1368373145277587235)
XLA Ops:
  9.9 42.7 %all-reduce.7 = (bf16[768]{0:T(1024)(128)(2,1)S(1)}, bf16[3072]{0:T(1024)(128)(2,1)S(1)}) all-reduce(bf16[768]{0:T(1024)(128)(2,1)S(1)} %dynamic-update-slice, bf16[3072]{0:T(1024)(128)(2,1)S(1)} %dynamic-update-slice.1), channel_id=1, replica_groups=mesh['seq'=4,'clip'=8] {'seq','clip'}, use_global_device_ids=true, to_apply=%add | all-reduce | flops 3840 | bytes 15360
  52.6 65.9 %all-gather = bf16[32,24,2]{1,2,0:T(2,128)(2,1)S(1)} all-gather(bf16[1,24,2]{1,2,0:T(2,128)(2,1)} %bitcast.197), channel_id=1, replica_groups=mesh['seq'=4,'clip'=8] {'seq','clip'}, dimensions={0}, use_global_device_ids=true | all-gather | bytes 3168 | tf_op jit(solution)/shard_map/all_gather | solution.py:143
  118.8 63.9 %all-gather.1 = bf16[32,24,6]{1,2,0:T(8,128)(2,1)S(1)} all-gather(bf16[1,24,6]{1,2,0:T(8,128)(2,1)} %bitcast.196), channel_id=1, replica_groups=mesh['seq'=4,'clip'=8] {'seq','clip'}, dimensions={0}, use_global_device_ids=true | all-gather | bytes 9504 | tf_op jit(solution)/shard_map/all_gather | solution.py:144
  192.0 6.4 fusion.35
  198.4 3.6 copy-done.16
  203.4 4.5 fusion.16
  212.2 35.7 %all-gather.13.cloned.1.call-done = bf16[8,8,64,768]{3,2,1,0:T(8,128)(2,1)} async-done(((bf16[8,8,16,768]{3,2,1,0:T(8,128)(2,1)}), bf16[8,8,64,768]{3,2,1,0:T(8,128)(2,1)}) %all-gather.13.cloned.1.call-update) | async-done | bytes 6291472 | tf_op jit(solution)/shard_map/all_gather | solution.py:178
  247.9 8.7 copy.90
  256.5 39.8 %all-gather.11.cloned.1.call-done = bf16[8,8,64,768]{3,2,1,0:T(8,128)(2,1)} async-done(((bf16[8,8,16,768]{3,2,1,0:T(8,128)(2,1)}), bf16[8,8,64,768]{3,2,1,0:T(8,128)(2,1)}) %all-gather.11.cloned.1.call-update) | async-done | bytes 6291472 | tf_op jit(solution)/shard_map/all_gather | solution.py:179
  296.4 8.6 copy.88
  305.0 30.4 %while.26 = (s32[]{:T(128)}, bf16[2,4,128,768]{3,2,1,0:T(8,128)(2,1)S(1)}, f32[2,4,12,128]{3,2,1,0:T(8,128)S(1)}, bf16[2,4,512,768]{2,3,1,0:T(8,128)(2,1)}, bf16...) while((s32[]{:T(128)}, bf16[2,4,128,768]{3,2,1,0:T(8,128)(2,1)S(1)}, ...), condition=%wide.region_6.7_spmd, body=%wide.region_3.6_spmd.sunk | while | flops 834004992 | bytes 63135844 | solution.py:185
  306.3 3.3 constant_dynamic-slice_fusion.15
  309.6 2.0 multiply_reduce_fusion.10
  311.6 3.1 fusion.90
  314.6 5.2 fusion.91
  321.5 3.3 constant_dynamic-slice_fusion.15
  324.7 2.0 multiply_reduce_fusion.10
  326.7 3.1 fusion.90
  329.8 5.2 fusion.91
  335.4 17.9 %all-gather.15.cloned.1.call-done = bf16[768,768]{1,0:T(8,128)(2,1)} async-done(((bf16[24,768]{1,0:T(8,128)(2,1)}), bf16[768,768]{1,0:T(8,128)(2,1)}) %all-gather.15.cloned.1.call-update) | async-done | bytes 1179664 | tf_op jit(solution)/shard_map/all_gather | solution.py:141
  353.3 3.9 fusion.33
  357.8 60.8 %all-gather.17.cloned.1.call-done = bf16[768,3072]{1,0:T(8,128)(2,1)} async-done(((bf16[24,3072]{1,0:T(8,128)(2,1)}), bf16[768,3072]{1,0:T(8,128)(2,1)}) %all-gather.17.cloned.1.call-update) | async-done | bytes 4718608 | tf_op jit(solution)/shard_map/all_gather | solution.py:145
  418.5 35.8 %multiply_convert_fusion.2 = (bf16[1024,3072]{1,0:T(8,128)(2,1)}, f32[1024,3072]{1,0:T(8,128)}, f32[1024,3072]{1,0:T(8,128)}) fusion(f32[3072]{0:T(1024)S(1)} %copy-done.51, bf16[768,3072]{1,0:T(8,128)(2,1)} %all-gather.17.cloned.1.call-done, f32[1024,768]{1,0:T(8,128)S(1)} %get-tuple-element.251, f32[768]{0:T(1024)S(1)} %copy-done.35, ...), kind=kOutput, calls=%fused_computation.34 | convolution fusion | flops 5043388416 | bytes 39348224 | tf_op jit(solution)/shard_map/dot_general | solution.py:192
  454.3 28.8 %all-gather.19.cloned.1.call-done = bf16[3072,768]{1,0:T(8,128)(2,1)} async-done(((bf16[96,768]{1,0:T(8,128)(2,1)}), bf16[3072,768]{1,0:T(8,128)(2,1)}) %all-gather.19.cloned.1.call-update) | async-done | bytes 4718608 | tf_op jit(solution)/shard_map/all_gather | solution.py:146
  483.1 19.3 %convert_reduce_fusion = (f32[3072]{0:T(1024)}, bf16[1024,3072]{1,0:T(8,128)(2,1)}) fusion(f32[1024,3072]{1,0:T(8,128)} %get-tuple-element.237, bf16[1024,768]{1,0:T(8,128)(2,1)} %bitcast.175, bf16[3072,768]{1,0:T(8,128)(2,1)} %all-gather.19.cloned.1.call-done, f32[1024,3072]{1,0:T(8,128)} %get-tuple-element.252, f32[3072]{0:T(1024)S(1)} %copy-done.51), kind=kOutput, calls=%fused_computation.32 | convolution fusion | flops 4885312512 | bytes 37773312 | tf_op jit(solution)/shard_map/dot_general | solution.py:29
  502.5 9.8 multiply_reduce_fusion.2
  515.9 2.6 convolution_convert_fusion
  518.5 115.8 %while.27 = (s32[]{:T(128)}, bf16[2,4,128,768]{2,3,1,0:T(8,128)(2,1)}, bf16[2,4,512,768]{3,2,1,0:T(8,128)(2,1)}, bf16[2,4,512,768]{3,2,1,0:T(8,128)(2,1)}, bf16[...) while((s32[]{:T(128)}, ...), condition=%wide.region_13.14_spmd, body=%wide.region_11.13_spmd.sunk | while | flops 2054940672 | bytes 306094400 | solution.py:217
  522.2 4.1 constant_dynamic-slice_fusion.20
  529.5 5.2 fusion.103
  534.9 4.7 copy.134
  539.6 12.5 multiply_reduce_fusion.11
  552.1 6.6 multiply_convert_fusion.5
  558.7 3.2 multiply_convert_fusion.6
  562.0 2.7 broadcast_multiply_fusion.4
  564.6 4.8 copy.135
  569.4 2.1 constant_dynamic-update-slice_fusion.8
  571.5 4.9 constant_dynamic-update-slice_fusion.9
  580.0 4.1 constant_dynamic-slice_fusion.20
  587.3 5.2 fusion.103
  592.7 4.7 copy.134
  597.4 12.5 multiply_reduce_fusion.11
  609.9 6.6 multiply_convert_fusion.5
  616.5 3.2 multiply_convert_fusion.6
  619.8 2.7 broadcast_multiply_fusion.4
  622.4 4.8 copy.135
  627.2 2.1 constant_dynamic-update-slice_fusion.8
  629.3 5.0 constant_dynamic-update-slice_fusion.9
  635.2 4.9 fusion.36
  640.2 12.3 fusion.27
  652.6 10.7 fusion.37
  663.3 2.8 copy.96
  666.1 24.6 %reduce-scatter.9.cloned.1.call-done = bf16[8,8,16,768]{3,2,1,0:T(8,128)(2,1)} async-done(((bf16[8,8,64,768]{3,2,1,0:T(8,128)(2,1)}), bf16[8,8,16,768]{3,2,1,0:T(8,128)(2,1)}) %reduce-scatter.9.cloned.1.call-update) | async-done | bytes 1572880 | tf_op jit(solution)/shard_map/reduce_scatter | solution.py:221
  690.7 60.5 %reduce-scatter.11.cloned.1.call-done = bf16[8,8,16,768]{3,2,1,0:T(8,128)(2,1)} async-done(((bf16[8,8,64,768]{3,2,1,0:T(8,128)(2,1)}), bf16[8,8,16,768]{3,2,1,0:T(8,128)(2,1)}) %reduce-scatter.11.cloned.1.call-update) | async-done | bytes 1572880 | tf_op jit(solution)/shard_map/reduce_scatter | solution.py:229
  751.1 9.6 fusion.22
  774.4 9.6 add_convert_fusion.1
  784.5 5.8 multiply_reduce_fusion.3
  790.4 3.2 fusion.30
  793.7 2.2 select_reduce_fusion
  796.0 40.3 %all-reduce.6 = (f32[768]{0:T(1024)S(1)}, f32[2,768]{1,0:T(2,128)S(1)}, f32[6,768]{1,0:T(8,128)S(1)}, f32[3072]{0:T(1024)S(1)}) all-reduce(f32[768]{0:T(1024)S(1)} %get-tuple-element.248, f32[2,768]{1,0:T(2,128)S(1)} %pad_maximum_fusion.3, f32[6,768]{1,0:T(8,128)S(1)} %stack.27, ...), channel_id=6, replica_groups=mesh['seq'=4,'clip'=8] {'seq','clip'}, use_global_device_ids=true, to_apply=%region_21.22.clone | all-reduce | flops 9984 | bytes 79872
  838.8 18.1 %reduce-scatter.15.cloned.1.call-done = f32[24,768]{1,0:T(8,128)} async-done(((f32[768,768]{1,0:T(8,128)}), f32[24,768]{1,0:T(8,128)}) %reduce-scatter.15.cloned.1.call-update) | async-done | bytes 73744 | tf_op jit(solution)/shard_map/reduce_scatter | solution.py:263
  856.9 141.5 %reduce-scatter.17.cloned.1.call-done = f32[24,3072]{1,0:T(8,128)} async-done(((f32[768,3072]{1,0:T(8,128)}), f32[24,3072]{1,0:T(8,128)}) %reduce-scatter.17.cloned.1.call-update) | async-done | bytes 294928 | tf_op jit(solution)/shard_map/reduce_scatter | solution.py:267
  998.4 141.7 %reduce-scatter.19.cloned.1.call-done = f32[96,768]{1,0:T(8,128)} async-done(((f32[3072,768]{1,0:T(8,128)}), f32[96,768]{1,0:T(8,128)}) %reduce-scatter.19.cloned.1.call-update) | async-done | bytes 294928 | tf_op jit(solution)/shard_map/reduce_scatter | solution.py:268
  1140.1 124.7 %reduce-scatter.13.cloned.1.call-done = f32[24,2304]{1,0:T(8,128)} async-done(((f32[768,2304]{1,0:T(8,128)}), f32[24,2304]{1,0:T(8,128)}) %reduce-scatter.13.cloned.1.call-update) | async-done | bytes 221200 | tf_op jit(solution)/shard_map/reduce_scatter | solution.py:262
  (253 shorter events, 56.2 us)
Async XLA Ops:
  7.2 181.5 %copy-start.11 = (bf16[8,8,16,768]{3,2,1,0:T(8,128)(2,1)S(1)}, bf16[8,8,16,768]{3,2,1,0:T(8,128)(2,1)}, u32[]{:S(2)}) copy-start(bf16[8,8,16,768]{3,2,1,0:T(8,128)(2,1)} %param.24) | copy-start | bytes 4718596
  7.2 184.8 %all-gather.9.cloned.1.call-start = ((), (), s32[]{:S(2)}) async-start(), calls=%async_computation.6 | async-start | bytes 3649536 | tf_op jit(solution)/shard_map/all_gather | solution.py:140
  7.9 239.9 %all-gather.13.cloned.1.call-start = ((), (), s32[]{:S(2)}) async-start(), calls=%async_computation.8 | async-start | bytes 7864320 | tf_op jit(solution)/shard_map/all_gather | solution.py:178
  52.6 139.4 %copy-start.30 = (f32[768]{0:T(1024)}, f32[768]{0:T(1024)S(1)}, u32[]{:S(2)}) copy-start(f32[768]{0:T(1024)S(1)} %convert_element_type.162) | copy-start | bytes 9220
  186.6 5.4 copy-start.47
  188.7 9.7 copy-start.37
  192.0 6.4 copy-start.18
  203.4 93.0 %all-gather.11.cloned.1.call-start = ((), (), s32[]{:S(2)}) async-start(), calls=%async_computation.7 | async-start | bytes 7864320 | tf_op jit(solution)/shard_map/all_gather | solution.py:179
  208.0 145.3 %all-gather.15.cloned.1.call-start = ((), (), s32[]{:S(2)}) async-start(), calls=%async_computation.9 | async-start | bytes 1216512 | tf_op jit(solution)/shard_map/all_gather | solution.py:141
  208.5 210.0 %all-gather.17.cloned.1.call-start = ((), (), s32[]{:S(2)}) async-start(), calls=%async_computation.10 | async-start | bytes 4866048 | tf_op jit(solution)/shard_map/all_gather | solution.py:145
  209.1 274.0 %all-gather.19.cloned.1.call-start = ((), (), s32[]{:S(2)}) async-start(), calls=%async_computation.11 | async-start | bytes 4866048 | tf_op jit(solution)/shard_map/all_gather | solution.py:146
  209.7 481.0 %reduce-scatter.9.cloned.1.call-start = ((), (), s32[]{:S(2)}) async-start(), calls=%async_computation.12 | async-start | bytes 7864320 | tf_op jit(solution)/shard_map/reduce_scatter | solution.py:221
  305.0 48.3 %copy-start.31 = (f32[768]{0:T(1024)S(1)}, f32[768]{0:T(1024)}, u32[]{:S(2)}) copy-start(f32[768]{0:T(1024)} %copy-done.30) | copy-start | bytes 9220
  305.0 48.3 %copy-start.48 = (pred[8,128]{1,0:T(8,128)(4,1)S(1)}, pred[8,128]{1,0:T(8,128)(4,1)}, u32[]{:S(2)}) copy-start(pred[8,128]{1,0:T(8,128)(4,1)} %copy-done.47) | copy-start | bytes 3076
  305.0 48.3 %copy-start.57 = (f32[768]{0:T(1024)S(1)}, f32[768]{0:T(1024)}, u32[]{:S(2)}) copy-start(f32[768]{0:T(1024)} %get-tuple-element.188) | copy-start | bytes 9220
  335.4 17.9 %copy-start.60 = (bf16[2,4,128,768]{3,2,1,0:T(8,128)(2,1)}, bf16[2,4,128,768]{3,2,1,0:T(8,128)(2,1)S(1)}, u32[]{:S(2)}) copy-start(bf16[2,4,128,768]{3,2,1,0:T(8,128)(2,1)S(1)} %get-tuple-element.100) | copy-start | bytes 4718596
  357.2 155.1 %copy-start.7 = (f32[1024,768]{1,0:T(8,128)}, f32[1024,768]{1,0:T(8,128)S(1)}, u32[]{:S(2)}) copy-start(f32[1024,768]{1,0:T(8,128)S(1)} %get-tuple-element.251) | copy-start | bytes 9437188
  357.2 61.3 %copy-start.33 = (f32[768]{0:T(1024)S(1)}, f32[768]{0:T(1024)}, u32[]{:S(2)}) copy-start(f32[768]{0:T(1024)} %get-tuple-element.192) | copy-start | bytes 9220
  357.2 61.3 %copy-start.35 = (f32[768]{0:T(1024)S(1)}, f32[768]{0:T(1024)}, u32[]{:S(2)}) copy-start(f32[768]{0:T(1024)} %get-tuple-element.187) | copy-start | bytes 9220
  357.2 61.3 %copy-start.51 = (f32[3072]{0:T(1024)S(1)}, f32[3072]{0:T(1024)}, u32[]{:S(2)}) copy-start(f32[3072]{0:T(1024)} %convert_element_type.172) | copy-start | bytes 36868
  357.2 155.0 %copy-start.25 = (f32[1024]{0:T(1024)}, f32[1024]{0:T(1024)S(1)}, u32[]{:S(2)}) copy-start(f32[1024]{0:T(1024)S(1)} %broadcast_multiply_fusion.2) | copy-start | bytes 12292
  357.7 154.5 %copy-start.28 = (f32[1024]{0:T(1024)}, f32[1024]{0:T(1024)S(1)}, u32[]{:S(2)}) copy-start(f32[1024]{0:T(1024)S(1)} %fusion.24) | copy-start | bytes 12292
  522.2 5.4 copy-start.5
  522.2 5.2 copy-start.4
  529.5 5.4 copy-start
  539.6 12.5 copy-start.1
  564.6 6.9 copy-start.2
  580.0 5.4 copy-start.5
  580.0 5.2 copy-start.4
  587.3 5.4 copy-start
  597.4 12.5 copy-start.1
  622.4 6.9 copy-start.2
  634.3 116.8 %reduce-scatter.11.cloned.1.call-start = ((), (), s32[]{:S(2)}) async-start(), calls=%async_computation.13 | async-start | bytes 7864320 | tf_op jit(solution)/shard_map/reduce_scatter | solution.py:229
  635.1 5.0 copy-start.8
  635.1 5.0 copy-start.26
  635.1 5.0 copy-start.29
  635.1 5.0 copy-start.34
  635.1 5.0 copy-start.36
  635.1 221.7 %reduce-scatter.15.cloned.1.call-start = ((), (), s32[]{:S(2)}) async-start(), calls=%async_computation.15 | async-start | bytes 2433024 | tf_op jit(solution)/shard_map/reduce_scatter | solution.py:263
  640.1 358.3 %reduce-scatter.17.cloned.1.call-start = ((), (), s32[]{:S(2)}) async-start(), calls=%async_computation.16 | async-start | bytes 9732096 | tf_op jit(solution)/shard_map/reduce_scatter | solution.py:267
  652.5 487.6 %reduce-scatter.19.cloned.1.call-start = ((), (), s32[]{:S(2)}) async-start(), calls=%async_computation.17 | async-start | bytes 9732096 | tf_op jit(solution)/shard_map/reduce_scatter | solution.py:268
  663.3 601.5 %reduce-scatter.13.cloned.1.call-start = ((), (), s32[]{:S(2)}) async-start(), calls=%async_computation.14 | async-start | bytes 7299072 | tf_op jit(solution)/shard_map/reduce_scatter | solution.py:262
  760.7 9.0 copy-start.22
  760.7 10.8 copy-start.24
  760.8 12.4 copy-start.23
  760.8 13.2 %copy-start.50 = (f32[768]{0:T(1024)S(1)}, f32[768]{0:T(1024)}, u32[]{:S(2)}) copy-start(f32[768]{0:T(1024)} %get-tuple-element.230) | copy-start | bytes 9220
  760.8 12.4 copy-start.27
  760.8 13.1 %copy-start.55 = (f32[768]{0:T(1024)S(1)}, f32[768]{0:T(1024)}, u32[]{:S(2)}) copy-start(f32[768]{0:T(1024)} %get-tuple-element.180) | copy-start | bytes 9220
  760.8 13.1 %copy-start.54 = (f32[768]{0:T(1024)S(1)}, f32[768]{0:T(1024)}, u32[]{:S(2)}) copy-start(f32[768]{0:T(1024)} %get-tuple-element.184) | copy-start | bytes 9220
  760.8 13.2 %copy-start.17 = (bf16[2,4,128,768]{2,3,1,0:T(8,128)(2,1)S(1)}, bf16[2,4,128,768]{2,3,1,0:T(8,128)(2,1)}, u32[]{:S(2)}) copy-start(bf16[2,4,128,768]{2,3,1,0:T(8,128)(2,1)} %get-tuple-element.102) | copy-start | bytes 4718596
  760.8 13.4 %copy-start.56 = (f32[768]{0:T(1024)S(1)}, f32[768]{0:T(1024)}, u32[]{:S(2)}) copy-start(f32[768]{0:T(1024)} %get-tuple-element.186) | copy-start | bytes 9220
  774.3 9.7 copy-start.19
  774.3 10.0 copy-start.12
  774.3 10.0 copy-start.20
  774.3 10.0 copy-start.32
  774.3 10.0 copy-start.38
  774.4 10.0 copy-start.40
  774.4 10.0 copy-start.42
  774.4 10.0 copy-start.49
  774.4 10.0 copy-start.58
  774.4 10.0 copy-start.59
  784.4 5.8 copy-start.53
  784.4 5.9 copy-start.46
  784.4 5.9 copy-start.13
  (17 other events, 39.4 us)
Sparse Core Ops, SparseCore 0:
  10.9 62.7 all-gather.8
  203.5 44.3 all-gather.12
  250.0 46.3 all-gather.10
  299.2 54.0 all-gather.14
  356.1 62.3 all-gather.16
  421.3 61.8 all-gather.18
  634.4 56.1 reduce-scatter.8
  693.2 57.8 reduce-scatter.10
  757.0 99.8 reduce-scatter.14
  863.2 135.1 reduce-scatter.16
  1004.9 135.1 reduce-scatter.18
  1146.2 118.5 reduce-scatter.12
where the time goes:
time: 1280 us; the launch traced here: 1270 us
  waiting for transfers between devices  697 us (54%)
  blocking collectives  213 us (17%)
  matrix products  196 us (15%)
  local copies, waits for them, and re-layouts  96.9 us (8%)
  other arithmetic  52.7 us (4%)
  between operations  15.5 us (1%)
    reduce_scatter x1, waiting for transfers between devices, body(): lax.psum_scatter(grad_down_part, ('seq', 'clip'), scatter_dimension=0, ti...  142 us
    reduce_scatter x1, waiting for transfers between devices, body(): lax.psum_scatter(grad_up_part, ('seq', 'clip'), scatter_dimension=0, tile...  142 us
    reduce_scatter x1, waiting for transfers between devices, body(): lax.psum_scatter(grad_qkv_part, ('seq', 'clip'), scatter_dimension=0, til...  125 us
    unnamed x2, blocking collectives  83 us
    all_gather x1, blocking collectives, body(): lax.all_gather(gains, ('seq', 'clip'), axis=1, tiled=True)  65.9 us
    all_gather x1, blocking collectives, body(): lax.all_gather(biases, ('seq', 'clip'), axis=1, tiled=True)  63.9 us
    all_gather x1, waiting for transfers between devices, body(): lax.all_gather(w_up, ('seq', 'clip'), axis=0, tiled=True)  60.8 us
    reduce_scatter x1, waiting for transfers between devices, body(): lax.psum_scatter(grad_value_groups.reshape(clip_count, freq_rows, time_to...  60.5 us
  transfers between devices with their start and end apart: 12, of which 11 were waited for; matrix products, arithmetic and copies ran while one was open for 14% of the time, Pallas kernels for 0%

commit v1 on v0

--- a/solution.py
+++ b/solution.py
@@ -7,6 +7,34 @@
 
 H = 12
 norm_eps = 1e-06
+
+
+def pairs_all_change(x_local):
+    a_name = "seq"
+    current_arr = lax.psum(1, a_name)
+    value_now = lax.axis_index(a_name)
+    tmp, row_out, mat_out = (current_arr, value_now, x_local.shape[2])
+    history = [p * tmp if ix == 2 else p for ix, p in enumerate(x_local.shape)]
+    item_now = lax.dynamic_update_slice_in_dim(
+        jnp.zeros(history, x_local.dtype), x_local, row_out * mat_out, axis=2
+    )
+    frame_out = arr_now = x_local
+    for m in range(1, tmp // 2 + 1):
+        a_next = map(lambda ix: (ix, (ix + 1) % tmp), range(tmp))
+        outcome_arr = list(a_next)
+        frame_out = lax.ppermute(frame_out, a_name, outcome_arr)
+        item_now = lax.dynamic_update_slice_in_dim(
+            item_now, frame_out, (row_out - m) % tmp * mat_out, axis=2
+        )
+        if 2 * m < tmp:
+            latest = range(tmp)
+            arr_now = lax.ppermute(
+                arr_now, a_name, list(map(lambda ix: (ix, (ix - 1) % tmp), latest))
+            )
+            item_now = lax.dynamic_update_slice_in_dim(
+                item_now, arr_now, (row_out + m) % tmp * mat_out, axis=2
+            )
+    return item_now
 
 
 def layer_norm(hidden, gain_row, shift_row):
@@ -175,7 +203,7 @@
     key_grid = keys_loc.reshape(grid_shape)
     value_grid = values_loc.reshape(grid_shape)
     key_all, value_all = (
-        lax.all_gather(key_grid, "seq", axis=2, tiled=True),
+        pairs_all_change(key_grid),
         lax.all_gather(value_grid, "seq", axis=2, tiled=True),
     )
     group_size = math.gcd(clip_count, max(1, 512 // local_len))

time: 1280 us -> 1260 us (0.984)
  waiting for transfers between devices: 697 us -> 659 us
  local copies, waits for them, and re-layouts: 96.9 us -> 110 us
    ppermute x0 -> x3, waiting for transfers between devices: none -> 66.7 us  [the longest x2 66.7 us: pairs_all_change(): frame_out = lax.ppermute(frame_out, a_name, outcome_arr)]
    all_gather x1, waiting for transfers between devices: 39.8 us -> 0.01 us  [body(): lax.all_gather(value_grid, 'seq', axis=2, tiled=True)]
    all_gather x1 -> x0, waiting for transfers between devices: 35.7 us -> none  [body(): lax.all_gather(key_grid, 'seq', axis=2, tiled=True)]
    all_gather x1, waiting for transfers between devices: 17.9 us -> 0.02 us  [body(): lax.all_gather(w_out, ('seq', 'clip'), axis=0, tiled=True)]
  transfers between devices with their start and end apart: 12 -> 14, of which waited for: 11 -> 10; matrix products, arithmetic and copies ran while one was open for 14% -> 16% of each run, Pallas kernels for 0% -> 0%
where the time goes in v1:
time: 1260 us; the launch traced here: 1250 us
  waiting for transfers between devices  659 us (52%)
  blocking collectives  213 us (17%)
  matrix products  196 us (16%)
  local copies, waits for them, and re-layouts  110 us (9%)
  other arithmetic  50.4 us (4%)
  between operations  15.2 us (1%)
    reduce_scatter x1, waiting for transfers between devices, body(): lax.psum_scatter(grad_up_part, ('seq', 'clip'), scatter_dimension=0, tile...  142 us
    reduce_scatter x1, waiting for transfers between devices, body(): lax.psum_scatter(grad_down_part, ('seq', 'clip'), scatter_dimension=0, ti...  141 us
    reduce_scatter x1, waiting for transfers between devices, body(): lax.psum_scatter(grad_qkv_part, ('seq', 'clip'), scatter_dimension=0, til...  125 us
    unnamed x2, blocking collectives  83 us
    ppermute x2, waiting for transfers between devices, pairs_all_change(): frame_out = lax.ppermute(frame_out, a_name, outcome_arr)  66.7 us
    all_gather x1, blocking collectives, body(): lax.all_gather(gains, ('seq', 'clip'), axis=1, tiled=True)  65.9 us
    all_gather x1, blocking collectives, body(): lax.all_gather(biases, ('seq', 'clip'), axis=1, tiled=True)  63.9 us
    reduce_scatter x1, waiting for transfers between devices, body(): lax.psum_scatter(grad_value_groups.reshape(clip_count, freq_rows, time_to...  60.5 us
  transfers between devices with their start and end apart: 14, of which 10 were waited for; matrix products, arithmetic and copies ran while one was open for 16% of the time, Pallas kernels for 0%

profile of v1, /device:TPU:0, one launch (start us, length us, event | category | flops | bytes accessed | tf_op | source)
XLA Modules:
  0.0 1252.2 jit_solution(16342992711686398186)
XLA Ops:
  9.9 42.7 %all-reduce.7 = (bf16[768]{0:T(1024)(128)(2,1)S(1)}, bf16[3072]{0:T(1024)(128)(2,1)S(1)}) all-reduce(bf16[768]{0:T(1024)(128)(2,1)S(1)} %dynamic-update-slice, bf16[3072]{0:T(1024)(128)(2,1)S(1)} %dynamic-update-slice.1), channel_id=1, replica_groups=mesh['seq'=4,'clip'=8] {'seq','clip'}, use_global_device_ids=true, to_apply=%add | all-reduce | flops 3840 | bytes 15360
  52.6 65.9 %all-gather = bf16[32,24,2]{1,2,0:T(2,128)(2,1)S(1)} all-gather(bf16[1,24,2]{1,2,0:T(2,128)(2,1)} %bitcast.198), channel_id=1, replica_groups=mesh['seq'=4,'clip'=8] {'seq','clip'}, dimensions={0}, use_global_device_ids=true | all-gather | bytes 3168 | tf_op jit(solution)/shard_map/all_gather | solution.py:171
  118.8 63.9 %all-gather.1 = bf16[32,24,6]{1,2,0:T(8,128)(2,1)S(1)} all-gather(bf16[1,24,6]{1,2,0:T(8,128)(2,1)} %bitcast.197), channel_id=1, replica_groups=mesh['seq'=4,'clip'=8] {'seq','clip'}, dimensions={0}, use_global_device_ids=true | all-gather | bytes 9504 | tf_op jit(solution)/shard_map/all_gather | solution.py:172
  192.0 6.4 fusion.35
  198.4 2.3 fusion.16
  207.8 61.1 %collective-permute-done = bf16[8,8,16,768]{3,2,1,0:T(8,128)(2,1)} collective-permute-done((bf16[8,8,16,768]{3,2,1,0:T(8,128)(2,1)S(1)}, bf16[8,8,16,768]{3,2,1,0:T(8,128)(2,1)}, u32[]{:S(2)}, u32[]{:S(2)}) %collective-permute-start) | collective-permute-done | bytes 1572896 | tf_op jit(solution)/shard_map/ppermute | solution.py:25
  268.8 6.4 collective-permute-start.2
  277.8 3.4 broadcast_in_dim.87
  282.5 2.7 constant_dynamic-update-slice_fusion.6
  285.2 2.7 constant_dynamic-update-slice_fusion.5
  287.9 5.7 collective-permute-done.2
  293.6 2.7 constant_dynamic-update-slice_fusion.4
  296.3 8.7 copy.93
  305.0 8.7 copy.91
  313.8 30.4 %while.26 = (s32[]{:T(128)}, bf16[2,4,128,768]{3,2,1,0:T(8,128)(2,1)S(1)}, f32[2,4,12,128]{3,2,1,0:T(8,128)S(1)}, bf16[2,4,512,768]{2,3,1,0:T(8,128)(2,1)}, bf16...) while((s32[]{:T(128)}, bf16[2,4,128,768]{3,2,1,0:T(8,128)(2,1)S(1)}, ...), condition=%wide.region_6.7_spmd, body=%wide.region_3.6_spmd.sunk | while | flops 834004992 | bytes 63135844 | solution.py:213
  315.0 3.3 constant_dynamic-slice_fusion.15
  320.2 3.1 fusion.90
  323.3 5.2 fusion.91
  330.1 3.3 constant_dynamic-slice_fusion.15
  335.4 3.1 fusion.90
  338.5 5.2 fusion.91
  345.3 3.9 fusion.33
  349.7 49.6 %all-gather.14.cloned.1.call-done = bf16[768,3072]{1,0:T(8,128)(2,1)} async-done(((bf16[24,3072]{1,0:T(8,128)(2,1)}), bf16[768,3072]{1,0:T(8,128)(2,1)}) %all-gather.14.cloned.1.call-update) | async-done | bytes 4718608 | tf_op jit(solution)/shard_map/all_gather | solution.py:173
  399.4 36.2 %multiply_convert_fusion.2 = (bf16[1024,3072]{1,0:T(8,128)(2,1)}, f32[1024,3072]{1,0:T(8,128)}, f32[1024,3072]{1,0:T(8,128)}) fusion(f32[3072]{0:T(1024)S(1)} %copy-done.51, bf16[768,3072]{1,0:T(8,128)(2,1)} %all-gather.14.cloned.1.call-done, f32[1024,768]{1,0:T(8,128)S(1)} %get-tuple-element.251, f32[768]{0:T(1024)S(1)} %copy-done.35, ...), kind=kOutput, calls=%fused_computation.34 | convolution fusion | flops 5043388416 | bytes 39348224 | tf_op jit(solution)/shard_map/dot_general | solution.py:220
  435.6 28.5 %all-gather.16.cloned.1.call-done = bf16[3072,768]{1,0:T(8,128)(2,1)} async-done(((bf16[96,768]{1,0:T(8,128)(2,1)}), bf16[3072,768]{1,0:T(8,128)(2,1)}) %all-gather.16.cloned.1.call-update) | async-done | bytes 4718608 | tf_op jit(solution)/shard_map/all_gather | solution.py:174
  464.1 18.7 %convert_reduce_fusion = (f32[3072]{0:T(1024)}, bf16[1024,3072]{1,0:T(8,128)(2,1)}) fusion(f32[1024,3072]{1,0:T(8,128)} %get-tuple-element.237, bf16[1024,768]{1,0:T(8,128)(2,1)} %bitcast.175, bf16[3072,768]{1,0:T(8,128)(2,1)} %all-gather.16.cloned.1.call-done, f32[1024,3072]{1,0:T(8,128)} %get-tuple-element.252, f32[3072]{0:T(1024)S(1)} %copy-done.51), kind=kOutput, calls=%fused_computation.32 | convolution fusion | flops 4885312512 | bytes 37773312 | tf_op jit(solution)/shard_map/dot_general | solution.py:57
  482.8 9.8 multiply_reduce_fusion.2
  496.3 2.6 convolution_convert_fusion
  498.8 115.8 %while.27 = (s32[]{:T(128)}, bf16[2,4,128,768]{2,3,1,0:T(8,128)(2,1)}, bf16[2,4,512,768]{3,2,1,0:T(8,128)(2,1)}, bf16[2,4,512,768]{3,2,1,0:T(8,128)(2,1)}, bf16[...) while((s32[]{:T(128)}, ...), condition=%wide.region_13.14_spmd, body=%wide.region_11.13_spmd.sunk | while | flops 2054940672 | bytes 306094400 | solution.py:245
  502.6 4.1 constant_dynamic-slice_fusion.20
  509.8 5.2 fusion.103
  515.2 4.7 copy.137
  520.0 12.5 multiply_reduce_fusion.11
  532.5 6.6 multiply_convert_fusion.5
  539.0 3.3 multiply_convert_fusion.6
  542.3 2.7 broadcast_multiply_fusion.4
  545.0 4.8 copy.138
  549.8 2.1 constant_dynamic-update-slice_fusion.12
  551.9 4.9 constant_dynamic-update-slice_fusion.13
  560.4 4.1 constant_dynamic-slice_fusion.20
  567.6 5.2 fusion.103
  573.0 4.7 copy.137
  577.8 12.5 multiply_reduce_fusion.11
  590.3 6.6 multiply_convert_fusion.5
  596.8 3.3 multiply_convert_fusion.6
  600.1 2.7 broadcast_multiply_fusion.4
  602.8 4.8 copy.138
  609.7 5.0 constant_dynamic-update-slice_fusion.13
  615.5 4.9 fusion.36
  620.5 12.3 fusion.27
  632.9 10.7 fusion.37
  643.7 2.8 copy.99
  646.4 24.6 %reduce-scatter.9.cloned.1.call-done = bf16[8,8,16,768]{3,2,1,0:T(8,128)(2,1)} async-done(((bf16[8,8,64,768]{3,2,1,0:T(8,128)(2,1)}), bf16[8,8,16,768]{3,2,1,0:T(8,128)(2,1)}) %reduce-scatter.9.cloned.1.call-update) | async-done | bytes 1572880 | tf_op jit(solution)/shard_map/reduce_scatter | solution.py:249
  671.0 60.5 %reduce-scatter.11.cloned.1.call-done = bf16[8,8,16,768]{3,2,1,0:T(8,128)(2,1)} async-done(((bf16[8,8,64,768]{3,2,1,0:T(8,128)(2,1)}), bf16[8,8,16,768]{3,2,1,0:T(8,128)(2,1)}) %reduce-scatter.11.cloned.1.call-update) | async-done | bytes 1572880 | tf_op jit(solution)/shard_map/reduce_scatter | solution.py:257
  731.5 9.6 fusion.22
  754.8 9.6 add_convert_fusion.1
  764.8 5.8 multiply_reduce_fusion.3
  770.7 3.2 fusion.30
  774.1 2.2 select_reduce_fusion
  776.4 40.3 %all-reduce.6 = (f32[768]{0:T(1024)S(1)}, f32[2,768]{1,0:T(2,128)S(1)}, f32[6,768]{1,0:T(8,128)S(1)}, f32[3072]{0:T(1024)S(1)}) all-reduce(f32[768]{0:T(1024)S(1)} %get-tuple-element.248, f32[2,768]{1,0:T(2,128)S(1)} %pad_maximum_fusion.3, f32[6,768]{1,0:T(8,128)S(1)} %stack.27, ...), channel_id=6, replica_groups=mesh['seq'=4,'clip'=8] {'seq','clip'}, use_global_device_ids=true, to_apply=%region_21.22.clone | all-reduce | flops 9984 | bytes 79872
  819.1 18.0 %reduce-scatter.15.cloned.1.call-done = f32[24,768]{1,0:T(8,128)} async-done(((f32[768,768]{1,0:T(8,128)}), f32[24,768]{1,0:T(8,128)}) %reduce-scatter.15.cloned.1.call-update) | async-done | bytes 73744 | tf_op jit(solution)/shard_map/reduce_scatter | solution.py:291
  837.2 141.8 %reduce-scatter.17.cloned.1.call-done = f32[24,3072]{1,0:T(8,128)} async-done(((f32[768,3072]{1,0:T(8,128)}), f32[24,3072]{1,0:T(8,128)}) %reduce-scatter.17.cloned.1.call-update) | async-done | bytes 294928 | tf_op jit(solution)/shard_map/reduce_scatter | solution.py:295
  979.0 141.5 %reduce-scatter.19.cloned.1.call-done = f32[96,768]{1,0:T(8,128)} async-done(((f32[3072,768]{1,0:T(8,128)}), f32[96,768]{1,0:T(8,128)}) %reduce-scatter.19.cloned.1.call-update) | async-done | bytes 294928 | tf_op jit(solution)/shard_map/reduce_scatter | solution.py:296
  1120.5 124.8 %reduce-scatter.13.cloned.1.call-done = f32[24,2304]{1,0:T(8,128)} async-done(((f32[768,2304]{1,0:T(8,128)}), f32[24,2304]{1,0:T(8,128)}) %reduce-scatter.13.cloned.1.call-update) | async-done | bytes 221200 | tf_op jit(solution)/shard_map/reduce_scatter | solution.py:290
  (263 shorter events, 68.7 us)
Async XLA Ops:
  7.2 181.5 %copy-start.11 = (bf16[8,8,16,768]{3,2,1,0:T(8,128)(2,1)S(1)}, bf16[8,8,16,768]{3,2,1,0:T(8,128)(2,1)}, u32[]{:S(2)}) copy-start(bf16[8,8,16,768]{3,2,1,0:T(8,128)(2,1)} %param.24) | copy-start | bytes 4718596
  7.2 184.8 %all-gather.8.cloned.1.call-start = ((), (), s32[]{:S(2)}) async-start(), calls=%async_computation.6 | async-start | bytes 3649536 | tf_op jit(solution)/shard_map/all_gather | solution.py:168
  7.9 297.1 %all-gather.10.cloned.1.call-start = ((), (), s32[]{:S(2)}) async-start(), calls=%async_computation.7 | async-start | bytes 7864320 | tf_op jit(solution)/shard_map/all_gather | solution.py:207
  52.6 139.4 %copy-start.30 = (f32[768]{0:T(1024)}, f32[768]{0:T(1024)S(1)}, u32[]{:S(2)}) copy-start(f32[768]{0:T(1024)S(1)} %convert_element_type.162) | copy-start | bytes 9220
  186.6 5.4 copy-start.47
  188.7 9.7 copy-start.37
  192.0 6.4 copy-start.18
  202.5 141.6 %all-gather.12.cloned.1.call-start = ((), (), s32[]{:S(2)}) async-start(), calls=%async_computation.8 | async-start | bytes 1216512 | tf_op jit(solution)/shard_map/all_gather | solution.py:169
  203.3 196.1 %all-gather.14.cloned.1.call-start = ((), (), s32[]{:S(2)}) async-start(), calls=%async_computation.9 | async-start | bytes 4866048 | tf_op jit(solution)/shard_map/all_gather | solution.py:173
  203.9 260.2 %all-gather.16.cloned.1.call-start = ((), (), s32[]{:S(2)}) async-start(), calls=%async_computation.10 | async-start | bytes 4866048 | tf_op jit(solution)/shard_map/all_gather | solution.py:174
  206.0 62.9 %collective-permute-start = (bf16[8,8,16,768]{3,2,1,0:T(8,128)(2,1)S(1)}, bf16[8,8,16,768]{3,2,1,0:T(8,128)(2,1)}, u32[]{:S(2)}, u32[]{:S(2)}) collective-permute-start(bf16[8,8,16,768]{3,2,1,0:T(8,128)(2,1)S(1)} %bitcast.180), channel_id=1, source_target_pairs={{0,8},{8,16},{16,24},{24,0},{1,9},{9,17},{17,25},{25,1},{2,10},{10... | collective-permute-start | bytes 4718600 | tf_op jit(solution)/shard_map/ppermute | solution.py:25
  206.0 79.2 %collective-permute-start.1 = (bf16[8,8,16,768]{3,2,1,0:T(8,128)(2,1)S(1)}, bf16[8,8,16,768]{3,2,1,0:T(8,128)(2,1)}, u32[]{:S(2)}, u32[]{:S(2)}) collective-permute-start(bf16[8,8,16,768]{3,2,1,0:T(8,128)(2,1)S(1)} %bitcast.181), channel_id=1, source_target_pairs={{0,24},{8,0},{16,8},{24,16},{1,25},{9,1},{17,9},{25,17},{2,26},{10... | collective-permute-start | bytes 4718600 | tf_op jit(solution)/shard_map/ppermute | solution.py:31
  268.8 24.8 %collective-permute-start.2 = (bf16[8,8,16,768]{3,2,1,0:T(8,128)(2,1)}, bf16[8,8,16,768]{3,2,1,0:T(8,128)(2,1)}, u32[]{:S(2)}, u32[]{:S(2)}) collective-permute-start(bf16[8,8,16,768]{3,2,1,0:T(8,128)(2,1)} %collective-permute-done), channel_id=1, source_target_pairs={{0,8},{8,16},{16,24},{24,0},{1,9},{9,17},{17,25},{25,1},{2,10},{10... | collective-permute-start | bytes 4718600 | tf_op jit(solution)/shard_map/ppermute | solution.py:25
  275.3 395.8 %reduce-scatter.9.cloned.1.call-start = ((), (), s32[]{:S(2)}) async-start(), calls=%async_computation.11 | async-start | bytes 7864320 | tf_op jit(solution)/shard_map/reduce_scatter | solution.py:249
  305.0 8.7 copy-start.60
  313.7 31.5 %copy-start.31 = (f32[768]{0:T(1024)S(1)}, f32[768]{0:T(1024)}, u32[]{:S(2)}) copy-start(f32[768]{0:T(1024)} %copy-done.30) | copy-start | bytes 9220
  313.7 31.5 %copy-start.48 = (pred[8,128]{1,0:T(8,128)(4,1)S(1)}, pred[8,128]{1,0:T(8,128)(4,1)}, u32[]{:S(2)}) copy-start(pred[8,128]{1,0:T(8,128)(4,1)} %copy-done.47) | copy-start | bytes 3076
  313.8 31.5 %copy-start.57 = (f32[768]{0:T(1024)S(1)}, f32[768]{0:T(1024)}, u32[]{:S(2)}) copy-start(f32[768]{0:T(1024)} %get-tuple-element.188) | copy-start | bytes 9220
  349.1 143.4 %copy-start.7 = (f32[1024,768]{1,0:T(8,128)}, f32[1024,768]{1,0:T(8,128)S(1)}, u32[]{:S(2)}) copy-start(f32[1024,768]{1,0:T(8,128)S(1)} %get-tuple-element.251) | copy-start | bytes 9437188
  349.2 50.2 %copy-start.33 = (f32[768]{0:T(1024)S(1)}, f32[768]{0:T(1024)}, u32[]{:S(2)}) copy-start(f32[768]{0:T(1024)} %get-tuple-element.192) | copy-start | bytes 9220
  349.2 50.2 %copy-start.35 = (f32[768]{0:T(1024)S(1)}, f32[768]{0:T(1024)}, u32[]{:S(2)}) copy-start(f32[768]{0:T(1024)} %get-tuple-element.187) | copy-start | bytes 9220
  349.2 50.2 %copy-start.51 = (f32[3072]{0:T(1024)S(1)}, f32[3072]{0:T(1024)}, u32[]{:S(2)}) copy-start(f32[3072]{0:T(1024)} %convert_element_type.172) | copy-start | bytes 36868
  349.2 143.4 %copy-start.25 = (f32[1024]{0:T(1024)}, f32[1024]{0:T(1024)S(1)}, u32[]{:S(2)}) copy-start(f32[1024]{0:T(1024)S(1)} %broadcast_multiply_fusion.2) | copy-start | bytes 12292
  349.7 142.9 %copy-start.28 = (f32[1024]{0:T(1024)}, f32[1024]{0:T(1024)S(1)}, u32[]{:S(2)}) copy-start(f32[1024]{0:T(1024)S(1)} %fusion.24) | copy-start | bytes 12292
  502.6 5.4 copy-start.5
  502.6 5.2 copy-start.4
  509.8 5.4 copy-start
  520.0 12.5 copy-start.1
  545.0 6.9 copy-start.2
  560.4 5.4 copy-start.5
  560.4 5.2 copy-start.4
  567.6 5.4 copy-start
  577.8 12.5 copy-start.1
  602.8 6.9 copy-start.2
  614.7 116.8 %reduce-scatter.11.cloned.1.call-start = ((), (), s32[]{:S(2)}) async-start(), calls=%async_computation.12 | async-start | bytes 7864320 | tf_op jit(solution)/shard_map/reduce_scatter | solution.py:257
  615.4 5.0 copy-start.8
  615.4 5.0 copy-start.26
  615.4 5.0 copy-start.29
  615.5 221.7 %reduce-scatter.15.cloned.1.call-start = ((), (), s32[]{:S(2)}) async-start(), calls=%async_computation.14 | async-start | bytes 2433024 | tf_op jit(solution)/shard_map/reduce_scatter | solution.py:291
  620.4 358.6 %reduce-scatter.17.cloned.1.call-start = ((), (), s32[]{:S(2)}) async-start(), calls=%async_computation.15 | async-start | bytes 9732096 | tf_op jit(solution)/shard_map/reduce_scatter | solution.py:295
  632.9 487.6 %reduce-scatter.19.cloned.1.call-start = ((), (), s32[]{:S(2)}) async-start(), calls=%async_computation.16 | async-start | bytes 9732096 | tf_op jit(solution)/shard_map/reduce_scatter | solution.py:296
  643.6 601.7 %reduce-scatter.13.cloned.1.call-start = ((), (), s32[]{:S(2)}) async-start(), calls=%async_computation.13 | async-start | bytes 7299072 | tf_op jit(solution)/shard_map/reduce_scatter | solution.py:290
  741.1 9.0 copy-start.22
  741.1 10.8 copy-start.24
  741.2 12.4 copy-start.23
  741.2 13.2 %copy-start.50 = (f32[768]{0:T(1024)S(1)}, f32[768]{0:T(1024)}, u32[]{:S(2)}) copy-start(f32[768]{0:T(1024)} %get-tuple-element.230) | copy-start | bytes 9220
  741.2 12.4 copy-start.27
  741.2 13.1 %copy-start.55 = (f32[768]{0:T(1024)S(1)}, f32[768]{0:T(1024)}, u32[]{:S(2)}) copy-start(f32[768]{0:T(1024)} %get-tuple-element.180) | copy-start | bytes 9220
  741.2 13.1 %copy-start.54 = (f32[768]{0:T(1024)S(1)}, f32[768]{0:T(1024)}, u32[]{:S(2)}) copy-start(f32[768]{0:T(1024)} %get-tuple-element.184) | copy-start | bytes 9220
  741.2 13.1 %copy-start.17 = (bf16[2,4,128,768]{2,3,1,0:T(8,128)(2,1)S(1)}, bf16[2,4,128,768]{2,3,1,0:T(8,128)(2,1)}, u32[]{:S(2)}) copy-start(bf16[2,4,128,768]{2,3,1,0:T(8,128)(2,1)} %get-tuple-element.102) | copy-start | bytes 4718596
  741.2 13.4 %copy-start.56 = (f32[768]{0:T(1024)S(1)}, f32[768]{0:T(1024)}, u32[]{:S(2)}) copy-start(f32[768]{0:T(1024)} %get-tuple-element.186) | copy-start | bytes 9220
  754.7 9.7 copy-start.19
  754.7 10.0 copy-start.12
  754.7 10.0 copy-start.20
  754.7 10.0 copy-start.32
  754.7 10.0 copy-start.38
  754.7 10.0 copy-start.40
  754.7 10.0 copy-start.42
  754.7 10.0 copy-start.49
  754.8 10.0 copy-start.58
  754.8 10.0 copy-start.59
  764.8 5.8 copy-start.53
  764.8 5.9 copy-start.46
  764.8 5.9 copy-start.13
  (20 other events, 51.1 us)
Sparse Core Ops, SparseCore 0:
  10.9 62.7 all-gather.7
  202.7 76.9 all-gather.9
  282.5 51.3 all-gather.11
  336.7 62.5 all-gather.13
  402.1 61.9 all-gather.15
  614.8 56.1 reduce-scatter.8
  673.6 57.9 reduce-scatter.10
  737.4 99.7 reduce-scatter.14
  843.6 135.2 reduce-scatter.16
  985.3 135.1 reduce-scatter.18
  1126.7 118.4 reduce-scatter.12
